TPU v7x, 32 devices: a whole 2x2x4 slice. The times are simulated.
32 devices in a mesh: groups: 2 (over y), seq: 4 (over z), head: 2 (over x), batch: 2 (over core).
Axes of the slice: x: 2, y: 2, z: 4, core: 2. Of those that a mesh axis runs over, the one named last changes fastest.
Arguments:
- queries: bfloat16 [4, 512, 2560], P(('groups', 'batch'), 'seq', 'head'), parts along dimension 0, may hold values from -6 to 6
- keys: bfloat16 [4, 512, 2560], P(('groups', 'batch'), 'seq', 'head'), parts along dimension 0, may hold values from -6 to 6
- values: bfloat16 [4, 512, 2560], P(('groups', 'batch'), 'seq', 'head'), parts along dimension 0, may hold values from -6 to 6
- cache_keys: bfloat16 [4, 8, 32, 2560], P(('groups', 'batch'), 'seq', None, 'head'), parts along dimension 0, may hold values from -6 to 6
- cache_values: bfloat16 [4, 8, 32, 2560], P(('groups', 'batch'), 'seq', None, 'head'), parts along dimension 0, may hold values from -6 to 6
- frame_list: int32 [4, 3], P(('groups', 'batch')), parts along dimension 0, may hold values from 0 to 7, as said below
- frame_place: int32 [4, 8], P(('groups', 'batch')), parts along dimension 0, may hold values from 0 to 7, each once within a row
- tile_mask: int32 [4, 4, 4], P(('groups', 'batch'), 'seq'), parts along dimension 0, may hold values from 0 to 1, as said below
Outputs:
- attention: bfloat16 [4, 512, 2560], P(('groups', 'batch'), 'seq', 'head'), parts along dimension 0
There are 2 independent parts, one for each index of `groups`. A program takes and returns all parts, laid end to end along the dimension named above; each array names one. Nothing has to cross between parts.
Inputs may be any that keep to these rules, and one draw needn't show every extreme that they name: `frame_list`: each row holds frame 0 and then 3 - 1 consecutive frame numbers. `tile_mask`: ones on the diagonal of each video's tile matrix.
All inputs are finite; a program needn't handle non-finite values.
Results may differ from a plain program's by a relative error of at most 0.006.
Values may be sent and summed in bfloat16 or wider, within the bound.
No kernel may reach another device: no remote copies, remote signals or barrier semaphores. Data moves between devices by JAX's collectives and lax.ppermute only.
A program may use at most 128 MiB of HBM per device.

v0:
```python
import math
import jax
import jax.numpy as jnp
from jax import lax
from jax.sharding import PartitionSpec as P

HD = 128
TILE = 128
NEG_FILL = -1e30


def attend(running, key_part, value_part, live, query_heads):
    videos, length, col_count = key_part.shape
    head_count = col_count // HD

    def update(previous):
        peak_old, total_old, summed_old = previous
        key_heads = key_part.reshape(videos, length, head_count, HD)
        value_heads = value_part.reshape(videos, length, head_count, HD)
        scores = jnp.einsum(
            "vqhd,vkhd->vhqk", query_heads, key_heads, preferred_element_type=jnp.float32
        ) * (1.0 / math.sqrt(HD))
        allowed = live[:, None, :, :]
        scores = jnp.where(allowed, scores, NEG_FILL)
        peak_new = jnp.maximum(peak_old, jnp.max(scores, axis=3))
        weights = jnp.where(allowed, jnp.exp(scores - peak_new[..., None]), 0.0)
        factor = jnp.exp(peak_old - peak_new)
        total_new = total_old * factor + jnp.sum(weights, axis=3)
        product = jnp.einsum(
            "vhqk,vkhd->vhqd",
            weights.astype(jnp.bfloat16),
            value_heads,
            preferred_element_type=jnp.float32,
        )
        summed_new = summed_old * factor[..., None] + product
        return (peak_new, total_new, summed_new)

    def unchanged(previous):
        return previous

    return lax.cond(jnp.any(live), update, unchanged, running)


def body(queries, keys, values, cache_keys, cache_values, frame_list, frame_place, tile_mask):
    videos, tok_rows, col_count = queries.shape
    head_count = col_count // HD
    query_heads = queries.reshape(videos, tok_rows, head_count, HD)
    running = (
        jnp.full((videos, head_count, tok_rows), NEG_FILL, jnp.float32),
        jnp.zeros((videos, head_count, tok_rows), jnp.float32),
        jnp.zeros((videos, head_count, tok_rows, HD), jnp.float32),
    )
    frame_tok = cache_keys.shape[2]
    listed = jnp.any(frame_place[:, :, None] == frame_list[:, None, :], axis=2)
    key_piece = lax.all_gather(cache_keys, "seq", axis=1, tiled=True)
    value_piece = lax.all_gather(cache_values, "seq", axis=1, tiled=True)
    count_frames = key_piece.shape[1]
    token_flags = jnp.repeat(listed, frame_tok, axis=1)
    live = jnp.broadcast_to(token_flags[:, None, :], (videos, tok_rows, count_frames * frame_tok))
    key_flat = key_piece.reshape(videos, count_frames * frame_tok, col_count)
    value_flat = value_piece.reshape(videos, count_frames * frame_tok, col_count)
    running = attend(running, key_flat, value_flat, live, query_heads)
    key_piece = lax.all_gather(keys, "seq", axis=1, tiled=True)
    value_piece = lax.all_gather(values, "seq", axis=1, tiled=True)
    length = key_piece.shape[1]
    key_tiles = jnp.arange(length, dtype=jnp.int32) // TILE
    tile_live = jnp.take(tile_mask, key_tiles, axis=2)
    running = attend(
        running, key_piece, value_piece, jnp.repeat(tile_live, TILE, axis=1) > 0, query_heads
    )
    peak, total, summed = running
    result = summed / total[..., None]
    return result.transpose(0, 2, 1, 3).reshape(videos, tok_rows, col_count).astype(jnp.bfloat16)


def solution(mesh):
    return jax.shard_map(
        body,
        mesh=mesh,
        in_specs=(
            P(("groups", "batch"), "seq", "head"),
            P(("groups", "batch"), "seq", "head"),
            P(("groups", "batch"), "seq", "head"),
            P(("groups", "batch"), "seq", None, "head"),
            P(("groups", "batch"), "seq", None, "head"),
            P(("groups", "batch"), None),
            P(("groups", "batch"), None),
            P(("groups", "batch"), "seq", None),
        ),
        out_specs=P(("groups", "batch"), "seq", "head"),
        check_vma=False,
    )
```

profile of v0, /device:TPU:0, one launch (start us, length us, event | category | flops | bytes accessed | tf_op | source)
XLA Modules:
  0.0 110.2 jit_solution(18014833076720647111)
XLA Ops:
  6.5 0.0 all-gather.3.cloned.1.call-start
  6.6 1.9 %copy.50 = bf16[1,128,1280]{1,2,0:T(8,128)(2,1)} copy(bf16[1,128,1280]{2,1,0:T(8,128)(2,1)} %param.13) | data formatting | bytes 655360 | tf_op args[1]
  8.5 0.0 all-gather.3.cloned.1.call-update
  8.6 0.0 all-gather.5.cloned.1.call-start
  8.6 1.9 %copy.51 = bf16[1,128,1280]{1,2,0:T(8,128)(2,1)} copy(bf16[1,128,1280]{2,1,0:T(8,128)(2,1)} %param.14) | data formatting | bytes 655360 | tf_op args[2]
  10.6 0.7 fusion.41
  11.2 2.7 %compare_select_fusion.1 = s32[512,1]{0,1:T(1,128)S(1)} fusion(s32[]{:T(128)} %bitcast.15, s32[]{:T(128)} %bitcast.16, s32[]{:T(128)} %bitcast.18, s32[]{:T(128)} %bitcast.17), kind=kLoop, calls=%fused_computation.45 | loop fusion | flops 8704 | bytes 2064 | tf_op jit(solution)/shard_map/jit(_take)/gather | solution.py:67
  14.0 0.8 broadcast_reduce_fusion
  15.4 0.1 compare_reduce_fusion
  15.5 0.1 broadcast_in_dim.88
  15.6 0.1 broadcast_in_dim.89
  15.7 0.7 broadcast_reduce_fusion.1
  17.2 0.2 copy.44
  17.4 27.2 %all_gather.12 = bf16[1,8,32,1280]{3,2,0,1:T(8,128)(2,1)S(1)} all-gather(bf16[1,2,32,1280]{3,2,0,1:T(8,128)(2,1)S(1)} %bitcast.73), channel_id=1, replica_groups=mesh['groups'=2,'seq'=4,'head'=2,'batch'=2] {'seq'}, dimensions={1}, use_global_device_ids=true | all-gather | bytes 819200 | tf_op jit(solution)/shard_map/all_gather | solution.py:55
  44.6 21.8 %all_gather.13 = bf16[1,8,32,1280]{3,2,0,1:T(8,128)(2,1)S(1)} all-gather(bf16[1,2,32,1280]{3,2,0,1:T(8,128)(2,1)S(1)} %bitcast.74), channel_id=1, replica_groups=mesh['groups'=2,'seq'=4,'head'=2,'batch'=2] {'seq'}, dimensions={1}, use_global_device_ids=true | all-gather | bytes 819200 | tf_op jit(solution)/shard_map/all_gather | solution.py:56
  66.3 3.3 %conditional.2 = (f32[1,10,128]{2,1,0:T(8,128)S(1)}, f32[1,10,128]{2,1,0:T(8,128)S(1)}, f32[1,10,128,128]{3,2,1,0:T(8,128)}) conditional(s32[]{:T(128)} %convert_element_type.32, () %tuple.20, (pred[8]{0:T(512)(128)(4,1)S(1)}, bf16[1,128,10,128]{1,3,2,0:T(8,128)(2,1)S(1)}, bf16[1,8,32,1280]{3,2,0,1:T(8,128)(2,1)S(1)}, ...), branch_computations={%region_3.4_spmd, %region_4.7_spmd} | conditional | flops 170891520 | bytes 8910368 | solution.py:41
  66.3 0.4 reshape.260
  66.7 0.1 broadcast_in_dim.71
  66.8 0.1 reshape.258
  66.9 0.5 fusion.40
  67.4 0.5 fusion.3
  67.9 0.4 reshape.261
  68.3 1.3 %fusion.1 = f32[1,10,128,128]{3,2,1,0:T(8,128)} fusion(f32[10,128,256]{2,1,0:T(8,128)S(1)} %get-tuple-element.99, bf16[256,10,128]{2,1,0:T(8,128)(2,1)S(1)} %reshape.261, f32[10,128]{1,0:T(8,128)S(1)} %get-tuple-element.97, pred[256]{0:T(512)(128)(4,1)S(1)} %reshape.258, f32[10,128]{1,0:T(8,128)S(1)} %get-tuple-element.96), kind=kOutput, calls=%fused_computation.4 | convolution fusion | flops 85032960 | bytes 2631936 | tf_op jit(solution)/shard_map/cond/branch_1_fun/vhqk,vkhd->vhqd/dot_general | solution.py:29
  69.6 26.9 %all-gather.5.cloned.1.call-done = bf16[1,512,1280]{1,2,0:T(8,128)(2,1)} async-done(((bf16[1,128,1280]{1,2,0:T(8,128)(2,1)}), bf16[1,512,1280]{1,2,0:T(8,128)(2,1)}) %all-gather.5.cloned.1.call-update) | async-done | bytes 1310736 | tf_op jit(solution)/shard_map/all_gather | solution.py:64
  96.6 5.8 %conditional.3 = (f32[1,10,128]{2,1,0:T(8,128)S(1)}, f32[1,10,128,128]{2,3,1,0:T(8,128)S(1)}) conditional(s32[]{:T(128)} %convert_element_type.31, (f32[1,10,128]{2,1,0:T(8,128)S(1)}, f32[1,10,128,128]{3,2,1,0:T(8,128)}) %tuple.22, (pred[1,128,512]{2,1,0:T(8,128)(4,1)S(1)}, bf16[1,128,10,128]{1,3,2,0:T(8,128)(2,1)S(1)}, ...), branch_computations={%region_7.8_spmd, %region_8.11_spmd} | conditional | flops 344396800 | bytes 18946092 | solution.py:41
  96.6 2.0 %fusion.13 = (f32[10,128]{1,0:T(8,128)S(1)}, f32[10,128,512]{2,1,0:T(8,128)S(1)}) fusion(pred[128,512]{1,0:T(8,128)(4,1)S(1)} %bitcast.70, bf16[512,10,128]{0,2,1:T(8,128)(2,1)} %bitcast.68, bf16[1,128,10,128]{1,3,2,0:T(8,128)(2,1)S(1)} %get-tuple-element.81), kind=kOutput, calls=%fused_computation.20 | convolution fusion | flops 169736960 | bytes 4330496 | tf_op jit(solution)/shard_map/cond/branch_1_fun/vqhd,vkhd->vhqk/dot_general | solution.py:20
  98.7 0.9 fusion.15
  99.5 0.4 copy-done.4
  100.0 2.2 %fusion.26 = f32[1,10,128,128]{3,2,1,0:T(8,128)S(1)} fusion(bf16[512,10,128]{0,2,1:T(8,128)(2,1)S(1)} %bitcast.77, f32[10,128,512]{2,1,0:T(8,128)S(1)} %get-tuple-element.95, f32[10,128]{1,0:T(8,128)S(1)} %get-tuple-element.93, pred[128,512]{1,0:T(8,128)(4,1)S(1)} %bitcast.72, f32[1,10,128,128]{3,2,1,0:T(8,128)} %get-tuple-element.42, ...), kind=kOutput, calls=%fused_computation.30 | convolution fusion | flops 171376640 | bytes 5318656 | tf_op jit(solution)/shard_map/cond/branch_1_fun/vhqk,vkhd->vhqd/dot_general | solution.py:29
  102.1 0.2 copy.58
  102.4 0.1 divide_convert_fusion
  102.4 0.9 copy.54
  (21 shorter events, 0.1 us)
Async XLA Ops:
  6.5 4.0 %copy-start.3 = (s32[1,1,4]{2,1,0:T(1,128)S(1)}, s32[1,1,4]{2,1,0:T(1,128)}, u32[]{:S(2)}) copy-start(s32[1,1,4]{2,1,0:T(1,128)} %param.19) | copy-start | bytes 52
  6.5 8.9 %copy-start.5 = (s32[1,8]{1,0:T(1,128)S(1)}, s32[1,8]{1,0:T(1,128)}, u32[]{:S(2)}) copy-start(s32[1,8]{1,0:T(1,128)} %param.18) | copy-start | bytes 100
  6.5 8.9 %copy-start.6 = (s32[1,3]{1,0:T(1,128)S(1)}, s32[1,3]{1,0:T(1,128)}, u32[]{:S(2)}) copy-start(s32[1,3]{1,0:T(1,128)} %param.17) | copy-start | bytes 40
  6.5 10.6 %copy-start = (bf16[1,128,1280]{2,1,0:T(8,128)(2,1)S(1)}, bf16[1,128,1280]{2,1,0:T(8,128)(2,1)}, u32[]{:S(2)}) copy-start(bf16[1,128,1280]{2,1,0:T(8,128)(2,1)} %param.12) | copy-start | bytes 983044
  6.5 10.8 %copy-start.1 = (bf16[1,2,32,1280]{3,2,1,0:T(8,128)(2,1)S(1)}, bf16[1,2,32,1280]{3,2,1,0:T(8,128)(2,1)}, u32[]{:S(2)}) copy-start(bf16[1,2,32,1280]{3,2,1,0:T(8,128)(2,1)} %param.15) | copy-start | bytes 491524
  6.5 63.1 %all-gather.3.cloned.1.call-start = ((), (), s32[]{:S(2)}) async-start(), calls=%async_computation | async-start | bytes 1638400 | tf_op jit(solution)/shard_map/all_gather | solution.py:63
  8.6 36.0 %copy-start.2 = (bf16[1,2,32,1280]{3,2,1,0:T(8,128)(2,1)S(1)}, bf16[1,2,32,1280]{3,2,1,0:T(8,128)(2,1)}, u32[]{:S(2)}) copy-start(bf16[1,2,32,1280]{3,2,1,0:T(8,128)(2,1)} %param.16) | copy-start | bytes 491524
  8.6 88.0 %all-gather.5.cloned.1.call-start = ((), (), s32[]{:S(2)}) async-start(), calls=%async_computation.1 | async-start | bytes 1638400 | tf_op jit(solution)/shard_map/all_gather | solution.py:64
  98.6 1.3 %copy-start.4 = (bf16[1,512,1280]{1,2,0:T(8,128)(2,1)S(1)}, bf16[1,512,1280]{1,2,0:T(8,128)(2,1)}, u32[]{:S(2)}) copy-start(bf16[1,512,1280]{1,2,0:T(8,128)(2,1)} %get-tuple-element.43) | copy-start | bytes 3932164 | tf_op jit(solution)/shard_map/cond
Sparse Core Ops, SparseCore 0:
  8.9 54.7 all-gather.2
  65.3 31.2 all-gather.4
where the time goes:
time: 111 us; the launch traced here: 110 us
  blocking collectives  49 us (44%)
  waiting for transfers between devices  27 us (24%)
  between operations  14.9 us (13%)
  local copies, waits for them, and re-layouts  7.46 us (7%)
  matrix products  5.99 us (5%)
  other arithmetic  5.75 us (5%)
    all_gather x1, blocking collectives, body(): key_piece = lax.all_gather(cache_keys, 'seq', axis=1, tiled=True)  27.2 us
    all_gather x1, waiting for transfers between devices, body(): value_piece = lax.all_gather(values, 'seq', axis=1, tiled=True)  26.9 us
    all_gather x1, blocking collectives, body(): value_piece = lax.all_gather(cache_values, 'seq', axis=1, tiled=True)  21.8 us
    unnamed x15, local copies, waits for them, and re-layouts  4.08 us
    dot_general x2, matrix products, update(): jnp.einsum('vhqk,vkhd->vhqd', weights.astype(jnp.bfloat16), value_heads,...  3.49 us
    gather x1, other arithmetic, body(): tile_live = jnp.take(tile_mask, key_tiles, axis=2)  2.7 us
    dot_general x2, matrix products, update(): jnp.einsum('vqhd,vkhd->vhqk', query_heads, key_heads, preferred_element_t...  2.5 us
  transfers between devices with their start and end apart: 2, of which 1 were waited for; matrix products, arithmetic and copies ran while one was open for 10% of the time, Pallas kernels for 0%

commit v1 on v0

--- a/solution.py
+++ b/solution.py
@@ -53,7 +53,19 @@
     frame_tok = cache_keys.shape[2]
     listed = jnp.any(frame_place[:, :, None] == frame_list[:, None, :], axis=2)
     key_piece = lax.all_gather(cache_keys, "seq", axis=1, tiled=True)
-    value_piece = lax.all_gather(cache_values, "seq", axis=1, tiled=True)
+    how_many = jax.lax.axis_size("seq")
+    by_rank = [(jj, (jj + 1) % how_many) for jj in range(how_many)]
+    pile = [(jj, (jj - 1) % how_many) for jj in range(how_many)]
+    shaped, high = ([cache_values], [cache_values])
+    for _ in range(how_many // 2):
+        block_last = jax.lax.ppermute(shaped[-1], perm=by_rank, axis_name="seq")
+        shaped.append(block_last)
+    for _ in tuple(range((how_many - 1) // 2)):
+        kept_arr = jax.lax.ppermute(high[-1], perm=pile, axis_name="seq")
+        high.append(kept_arr)
+    t1 = jnp.concatenate([*shaped[::-1], *high[1:]], axis=1)
+    y2 = jax.lax.axis_index("seq")
+    value_piece = jnp.roll(t1, (y2 - how_many // 2) * cache_values.shape[1], axis=1)
     count_frames = key_piece.shape[1]
     token_flags = jnp.repeat(listed, frame_tok, axis=1)
     live = jnp.broadcast_to(token_flags[:, None, :], (videos, tok_rows, count_frames * frame_tok))

time: 111 us -> 106 us (0.955)
  blocking collectives: 49 us -> 24.5 us
  waiting for transfers between devices: 27 us -> 36.9 us
  starting transfers between devices: 0.08 us -> 7.8 us
  local copies, waits for them, and re-layouts: 7.46 us -> 9.65 us
    all_gather x1 -> x0, blocking collectives: 21.8 us -> none  [body(): value_piece = lax.all_gather(cache_values, 'seq', axis=1, tiled=True)]
    ppermute x0 -> x3, starting transfers between devices: none -> 7.72 us  [the longest x2 5.63 us: body(): block_last = jax.lax.ppermute(shaped[-1], perm=by_rank, axis_name='seq')]
    all_gather x1, waiting for transfers between devices: 26.9 us -> 32 us  [body(): value_piece = lax.all_gather(values, 'seq', axis=1, tiled=True)]
    ppermute x0 -> x3, waiting for transfers between devices: none -> 4.92 us  [the longest x2 4.92 us: body(): block_last = jax.lax.ppermute(shaped[-1], perm=by_rank, axis_name='seq')]
    all_gather x1, blocking collectives: 27.2 us -> 24.5 us  [body(): key_piece = lax.all_gather(cache_keys, 'seq', axis=1, tiled=True)]
    dynamic_slice x0 -> x1, local copies, waits for them, and re-layouts: none -> 1.13 us  [body(): jnp.roll(t1, (y2 - how_many // 2) * cache_values.shape[1], axis=1)]
    unnamed x15 -> x22, local copies, waits for them, and re-layouts: 4.08 us -> 4.15 us
  transfers between devices with their start and end apart: 2 -> 5, of which waited for: 1 -> 2; matrix products, arithmetic and copies ran while one was open for 10% -> 11% of each run, Pallas kernels for 0% -> 0%
where the time goes in v1:
time: 106 us; the launch traced here: 105 us
  waiting for transfers between devices  36.9 us (35%)
  blocking collectives  24.5 us (23%)
  between operations  14.9 us (14%)
  local copies, waits for them, and re-layouts  9.65 us (9%)
  starting transfers between devices  7.8 us (7%)
  matrix products  5.99 us (6%)
  other arithmetic  5.53 us (5%)
    all_gather x1, waiting for transfers between devices, body(): value_piece = lax.all_gather(values, 'seq', axis=1, tiled=True)  32 us
    all_gather x1, blocking collectives, body(): key_piece = lax.all_gather(cache_keys, 'seq', axis=1, tiled=True)  24.5 us
    ppermute x2, starting transfers between devices, body(): block_last = jax.lax.ppermute(shaped[-1], perm=by_rank, axis_name='seq')  5.63 us
    ppermute x2, waiting for transfers between devices, body(): block_last = jax.lax.ppermute(shaped[-1], perm=by_rank, axis_name='seq')  4.92 us
    unnamed x22, local copies, waits for them, and re-layouts  4.15 us
    dot_general x2, matrix products, update(): jnp.einsum('vhqk,vkhd->vhqd', weights.astype(jnp.bfloat16), value_heads,...  3.49 us
    gather x1, other arithmetic, body(): tile_live = jnp.take(tile_mask, key_tiles, axis=2)  2.51 us
    dot_general x2, matrix products, update(): jnp.einsum('vqhd,vkhd->vhqk', query_heads, key_heads, preferred_element_t...  2.49 us
  transfers between devices with their start and end apart: 5, of which 2 were waited for; matrix products, arithmetic and copies ran while one was open for 11% of the time, Pallas kernels for 0%

profile of v1, /device:TPU:0, one launch (start us, length us, event | category | flops | bytes accessed | tf_op | source)
XLA Modules:
  0.0 105.4 jit_solution(15334325176263623631)
XLA Ops:
  6.6 2.0 %copy.45 = bf16[1,128,1280]{1,2,0:T(8,128)(2,1)} copy(bf16[1,128,1280]{2,1,0:T(8,128)(2,1)} %param.13) | data formatting | bytes 655360 | tf_op args[1]
  8.6 3.1 %collective-permute-start = (bf16[1,2,32,1280]{3,2,1,0:T(8,128)(2,1)}, bf16[1,2,32,1280]{3,2,1,0:T(8,128)(2,1)S(1)}, u32[]{:S(2)}, u32[]{:S(2)}) collective-permute-start(bf16[1,2,32,1280]{3,2,1,0:T(8,128)(2,1)} %param.16), channel_id=1, source_target_pairs={{0,4},{4,8},{8,12},{12,0},{1,5},{5,9},{9,13},{13,1},{2,6},{6,10},{... | collective-permute-start | bytes 491528 | tf_op jit(solution)/shard_map/ppermute | solution.py:61
  11.7 2.1 %collective-permute-start.2 = (bf16[1,2,32,1280]{3,2,1,0:T(8,128)(2,1)}, bf16[1,2,32,1280]{3,2,1,0:T(8,128)(2,1)S(1)}, u32[]{:S(2)}, u32[]{:S(2)}) collective-permute-start(bf16[1,2,32,1280]{3,2,1,0:T(8,128)(2,1)} %param.16), channel_id=1, source_target_pairs={{0,12},{4,0},{8,4},{12,8},{1,13},{5,1},{9,5},{13,9},{2,14},{6,2},{... | collective-permute-start | bytes 491528 | tf_op jit(solution)/shard_map/ppermute | solution.py:64
  13.8 1.9 %copy.46 = bf16[1,128,1280]{1,2,0:T(8,128)(2,1)} copy(bf16[1,128,1280]{2,1,0:T(8,128)(2,1)} %param.14) | data formatting | bytes 655360 | tf_op args[2]
  15.7 0.7 fusion.41
  16.4 24.5 %all_gather.9 = bf16[1,8,32,1280]{3,2,0,1:T(8,128)(2,1)S(1)} all-gather(bf16[1,2,32,1280]{3,2,0,1:T(8,128)(2,1)S(1)} %bitcast.70), channel_id=1, replica_groups=mesh['groups'=2,'seq'=4,'head'=2,'batch'=2] {'seq'}, dimensions={1}, use_global_device_ids=true | all-gather | bytes 819200 | tf_op jit(solution)/shard_map/all_gather | solution.py:55
  40.8 2.5 %compare_select_fusion.1 = s32[512,1]{0,1:T(1,128)S(1)} fusion(s32[]{:T(128)} %bitcast.14, s32[]{:T(128)} %bitcast.15, s32[]{:T(128)} %bitcast.17, s32[]{:T(128)} %bitcast.16), kind=kLoop, calls=%fused_computation.54 | loop fusion | flops 8704 | bytes 2064 | tf_op jit(solution)/shard_map/jit(_take)/gather | solution.py:79
  43.4 0.1 compare_reduce_fusion
  43.5 2.6 %collective-permute-start.1 = (bf16[1,2,32,1280]{3,2,1,0:T(8,128)(2,1)S(1)}, bf16[1,2,32,1280]{3,2,1,0:T(8,128)(2,1)S(1)}, u32[]{:S(2)}, u32[]{:S(2)}) collective-permute-start(bf16[1,2,32,1280]{3,2,1,0:T(8,128)(2,1)S(1)} %collective-permute-done), channel_id=1, source_target_pairs={{0,4},{4,8},{8,12},{12,0},{1,5},{5,9},{9,13},{13,1},{2,6},{6,10},{... | collective-permute-start | bytes 491528 | tf_op jit(solution)/shard_map/ppermute | solution.py:61
  46.0 0.8 broadcast_reduce_fusion
  47.5 0.1 broadcast_in_dim.86
  47.6 0.1 broadcast_in_dim.87
  47.6 0.7 broadcast_reduce_fusion.1
  49.1 0.2 copy.41
  49.3 4.9 %collective-permute-done.1 = bf16[1,2,32,1280]{3,2,1,0:T(8,128)(2,1)S(1)} collective-permute-done((bf16[1,2,32,1280]{3,2,1,0:T(8,128)(2,1)S(1)}, bf16[1,2,32,1280]{3,2,1,0:T(8,128)(2,1)S(1)}, u32[]{:S(2)}, u32[]{:S(2)}) %collective-permute-start.1) | collective-permute-done | bytes 163872 | tf_op jit(solution)/shard_map/ppermute | solution.py:61
  54.4 5.4 %conditional.2 = (f32[1,10,128]{2,1,0:T(8,128)S(1)}, f32[1,10,128]{2,1,0:T(8,128)S(1)}, f32[1,10,128,128]{3,2,1,0:T(8,128)}) conditional(s32[]{:T(128)} %convert_element_type.35, () %tuple.31, (pred[8,32]{1,0:T(8,128)(4,1)S(1)}, bf16[1,128,10,128]{1,3,2,0:T(8,128)(2,1)S(1)}, bf16[1,8,32,1280]{3,2,0,1:T(8,128)(2,1)S(1)}, s32[]{:T(128)}, s32[]{:T(128)}, ...), branch_computations={%region_3.4_spmd, %region_4.7_spmd} | conditional | flops 170891520 | bytes 15463891 | solution.py:41
  54.4 1.0 copy-done.1
  55.5 0.4 reshape.286
  55.9 0.1 reshape.284
  55.9 0.5 fusion.40
  56.4 0.5 fusion.3
  56.9 1.1 %constant_dynamic-slice_fusion = bf16[1,8,32,1280]{3,2,1,0:T(8,128)(2,1)S(1)} fusion(bf16[1,16,32,1280]{3,2,1,0:T(8,128)(2,1)} %copy-done.1, s32[]{:T(128)S(6)} %select_n.78), kind=kLoop, calls=%fused_computation.16 | loop fusion | bytes 1310724 | tf_op jit(solution)/shard_map/jit(_roll_dynamic)/dynamic_slice | solution.py:68
  58.1 0.4 reshape.287
  58.5 1.3 %fusion.1 = f32[1,10,128,128]{3,2,1,0:T(8,128)} fusion(f32[10,128,256]{2,1,0:T(8,128)S(1)} %get-tuple-element.208, bf16[256,10,128]{2,1,0:T(8,128)(2,1)S(1)} %reshape.287, f32[10,128]{1,0:T(8,128)S(1)} %get-tuple-element.206, pred[256]{0:T(512)(128)(4,1)S(1)} %reshape.284, f32[10,128]{1,0:T(8,128)S(1)} %get-tuple-element.205), kind=kOutput, calls=%fused_computation.4 | convolution fusion | flops 85032960 | bytes 2631936 | tf_op jit(solution)/shard_map/cond/branch_1_fun/vhqk,vkhd->vhqd/dot_general | solution.py:29
  59.8 32.0 %all-gather.5.cloned.1.call-done = bf16[1,512,1280]{1,2,0:T(8,128)(2,1)} async-done(((bf16[1,128,1280]{1,2,0:T(8,128)(2,1)}), bf16[1,512,1280]{1,2,0:T(8,128)(2,1)}) %all-gather.5.cloned.1.call-update) | async-done | bytes 1310736 | tf_op jit(solution)/shard_map/all_gather | solution.py:76
  91.8 5.8 %conditional.3 = (f32[1,10,128]{2,1,0:T(8,128)S(1)}, f32[1,10,128,128]{2,3,1,0:T(8,128)S(1)}) conditional(s32[]{:T(128)} %convert_element_type.34, (f32[1,10,128]{2,1,0:T(8,128)S(1)}, f32[1,10,128,128]{3,2,1,0:T(8,128)}) %tuple.33, (pred[1,128,512]{2,1,0:T(8,128)(4,1)S(1)}, bf16[1,128,10,128]{1,3,2,0:T(8,128)(2,1)S(1)}, ...), branch_computations={%region_7.8_spmd, %region_8.11_spmd} | conditional | flops 344396800 | bytes 18946092 | solution.py:41
  91.8 2.0 %fusion.13 = (f32[10,128]{1,0:T(8,128)S(1)}, f32[10,128,512]{2,1,0:T(8,128)S(1)}) fusion(pred[128,512]{1,0:T(8,128)(4,1)S(1)} %bitcast.67, bf16[512,10,128]{0,2,1:T(8,128)(2,1)} %bitcast.65, bf16[1,128,10,128]{1,3,2,0:T(8,128)(2,1)S(1)} %get-tuple-element.188), kind=kOutput, calls=%fused_computation.21 | convolution fusion | flops 169736960 | bytes 4330496 | tf_op jit(solution)/shard_map/cond/branch_1_fun/vqhd,vkhd->vhqk/dot_general | solution.py:20
  93.9 0.9 fusion.15
  94.8 0.4 copy-done.5
  95.2 2.2 %fusion.26 = f32[1,10,128,128]{3,2,1,0:T(8,128)S(1)} fusion(bf16[512,10,128]{0,2,1:T(8,128)(2,1)S(1)} %bitcast.73, f32[10,128,512]{2,1,0:T(8,128)S(1)} %get-tuple-element.204, f32[10,128]{1,0:T(8,128)S(1)} %get-tuple-element.202, pred[128,512]{1,0:T(8,128)(4,1)S(1)} %bitcast.69, f32[1,10,128,128]{3,2,1,0:T(8,128)} %get-tuple-element.128, ...), kind=kOutput, calls=%fused_computation.31 | convolution fusion | flops 171376640 | bytes 5318656 | tf_op jit(solution)/shard_map/cond/branch_1_fun/vhqk,vkhd->vhqd/dot_general | solution.py:29
  97.4 0.2 copy.53
  97.7 0.9 copy.49
  (36 shorter events, 0.4 us)
Async XLA Ops:
  6.5 9.2 %copy-start.4 = (s32[1,1,4]{2,1,0:T(1,128)S(1)}, s32[1,1,4]{2,1,0:T(1,128)}, u32[]{:S(2)}) copy-start(s32[1,1,4]{2,1,0:T(1,128)} %param.19) | copy-start | bytes 52
  6.5 9.8 %copy-start.3 = (bf16[1,2,32,1280]{3,2,1,0:T(8,128)(2,1)S(1)}, bf16[1,2,32,1280]{3,2,1,0:T(8,128)(2,1)}, u32[]{:S(2)}) copy-start(bf16[1,2,32,1280]{3,2,1,0:T(8,128)(2,1)} %param.15) | copy-start | bytes 491524
  6.5 36.8 %copy-start.6 = (s32[1,8]{1,0:T(1,128)S(1)}, s32[1,8]{1,0:T(1,128)}, u32[]{:S(2)}) copy-start(s32[1,8]{1,0:T(1,128)} %param.18) | copy-start | bytes 100
  6.5 36.8 %copy-start.7 = (s32[1,3]{1,0:T(1,128)S(1)}, s32[1,3]{1,0:T(1,128)}, u32[]{:S(2)}) copy-start(s32[1,3]{1,0:T(1,128)} %param.17) | copy-start | bytes 40
  6.5 42.5 %copy-start.2 = (bf16[1,128,1280]{2,1,0:T(8,128)(2,1)S(1)}, bf16[1,128,1280]{2,1,0:T(8,128)(2,1)}, u32[]{:S(2)}) copy-start(bf16[1,128,1280]{2,1,0:T(8,128)(2,1)} %param.12) | copy-start | bytes 983044
  6.5 53.3 %all-gather.3.cloned.1.call-start = ((), (), s32[]{:S(2)}) async-start(), calls=%async_computation | async-start | bytes 1638400 | tf_op jit(solution)/shard_map/all_gather | solution.py:75
  8.6 83.2 %all-gather.5.cloned.1.call-start = ((), (), s32[]{:S(2)}) async-start(), calls=%async_computation.1 | async-start | bytes 1638400 | tf_op jit(solution)/shard_map/all_gather | solution.py:76
  8.6 34.8 %collective-permute-start = (bf16[1,2,32,1280]{3,2,1,0:T(8,128)(2,1)}, bf16[1,2,32,1280]{3,2,1,0:T(8,128)(2,1)S(1)}, u32[]{:S(2)}, u32[]{:S(2)}) collective-permute-start(bf16[1,2,32,1280]{3,2,1,0:T(8,128)(2,1)} %param.16), channel_id=1, source_target_pairs={{0,4},{4,8},{8,12},{12,0},{1,5},{5,9},{9,13},{13,1},{2,6},{6,10},{... | collective-permute-start | bytes 491528 | tf_op jit(solution)/shard_map/ppermute | solution.py:61
  11.7 42.6 %collective-permute-start.2 = (bf16[1,2,32,1280]{3,2,1,0:T(8,128)(2,1)}, bf16[1,2,32,1280]{3,2,1,0:T(8,128)(2,1)S(1)}, u32[]{:S(2)}, u32[]{:S(2)}) collective-permute-start(bf16[1,2,32,1280]{3,2,1,0:T(8,128)(2,1)} %param.16), channel_id=1, source_target_pairs={{0,12},{4,0},{8,4},{12,8},{1,13},{5,1},{9,5},{13,9},{2,14},{6,2},{... | collective-permute-start | bytes 491528 | tf_op jit(solution)/shard_map/ppermute | solution.py:64
  15.7 38.6 %copy-start = (bf16[1,2,32,1280]{3,2,1,0:T(8,128)(2,1)S(1)}, bf16[1,2,32,1280]{3,2,1,0:T(8,128)(2,1)}, u32[]{:S(2)}) copy-start(bf16[1,2,32,1280]{3,2,1,0:T(8,128)(2,1)} %param.16) | copy-start | bytes 491524
  43.5 10.7 %collective-permute-start.1 = (bf16[1,2,32,1280]{3,2,1,0:T(8,128)(2,1)S(1)}, bf16[1,2,32,1280]{3,2,1,0:T(8,128)(2,1)S(1)}, u32[]{:S(2)}, u32[]{:S(2)}) collective-permute-start(bf16[1,2,32,1280]{3,2,1,0:T(8,128)(2,1)S(1)} %collective-permute-done), channel_id=1, source_target_pairs={{0,4},{4,8},{8,12},{12,0},{1,5},{5,9},{9,13},{13,1},{2,6},{6,10},{... | collective-permute-start | bytes 491528 | tf_op jit(solution)/shard_map/ppermute | solution.py:61
  54.4 1.1 %copy-start.1 = (bf16[1,16,32,1280]{3,2,1,0:T(8,128)(2,1)}, bf16[1,16,32,1280]{3,2,1,0:T(8,128)(2,1)S(1)}, u32[]{:S(2)}) copy-start(bf16[1,16,32,1280]{3,2,1,0:T(8,128)(2,1)S(1)} %get-tuple-element.120) | copy-start | bytes 3932164 | tf_op jit(solution)/shard_map/cond
  93.9 1.3 %copy-start.5 = (bf16[1,512,1280]{1,2,0:T(8,128)(2,1)S(1)}, bf16[1,512,1280]{1,2,0:T(8,128)(2,1)}, u32[]{:S(2)}) copy-start(bf16[1,512,1280]{1,2,0:T(8,128)(2,1)} %get-tuple-element.129) | copy-start | bytes 3932164 | tf_op jit(solution)/shard_map/cond
Sparse Core Ops, SparseCore 0:
  8.9 49.2 all-gather.2
  59.8 31.9 all-gather.4
